TPU v7x, 32 devices: a whole 2x2x4 slice. The times are simulated.
32 devices in a mesh: dp: 2 (over x), row: 4 (over z), col: 4 (over y, core).
Axes of the slice: x: 2, y: 2, z: 4, core: 2. Of those that a mesh axis runs over, the one named last changes fastest.
Arguments:
- hidden: bfloat16 [8192, 896], P(('dp', 'row'), 'col'), may hold values from -6 to 6
- segments: int32 [2, 4, 4, 256], P('dp', 'col', 'row'), may hold values from 0 to 3, never falling along the last dimension, each value on 1 to 128 neighbouring positions
- attn_gain: bfloat16 [2, 896], P(None, 'col'), may hold values from 0.5 to 1.5
- qkv_weight: bfloat16 [2, 896, 1152], P(None, 'col', 'row'), as said below
- qkv_bias: bfloat16 [2, 1152], P(None, 'row'), may hold values from -3 to 3
- out_weight: bfloat16 [2, 896, 896], P(None, 'row', 'col'), may hold values from -0.09375 to 0.09375
- mlp_gain: bfloat16 [2, 896], P(None, 'col'), may hold values from 0.5 to 1.5
- gate_up_weight: bfloat16 [2, 896, 2, 4864], P(None, 'col', None, 'row'), may hold values from -0.1875 to 0.1875
- down_weight: bfloat16 [2, 4864, 896], P(None, 'row', 'col'), may hold values from -0.15625 to 0.15625
- cotangent: bfloat16 [8192, 896], P(('dp', 'row'), 'col'), may hold values from -6 to 6
Outputs:
- result: bfloat16 [8192, 896], P(('dp', 'row'), 'col')
- grad_hidden: float32 [8192, 896], P(('dp', 'row'), 'col')
- attn_gain_grad: float32 [2, 896], P(None, 'col')
- qkv_weight_grad: float32 [2, 896, 1152], P(None, 'col', 'row')
- qkv_bias_grad: float32 [2, 1152], P(None, 'row')
- out_weight_grad: float32 [2, 896, 896], P(None, 'row', 'col')
- mlp_gain_grad: float32 [2, 896], P(None, 'col')
- gate_up_grad: float32 [2, 896, 2, 4864], P(None, 'col', None, 'row')
- down_grad: float32 [2, 4864, 896], P(None, 'row', 'col')
Inputs may be any that keep to these rules, and one draw needn't show every extreme that they name: `segments`: along each packed sequence of 256 tokens the numbers never fall; each number covers at most 128 tokens, and some covers exactly that many. `qkv_weight`: entries lie within 48 * 896 ** -0.5 in magnitude.
All inputs are finite; a program needn't handle non-finite values.
Results may differ from a plain program's by a relative error of at most 0.023.
Values may be sent and summed in bfloat16 or wider, within the bound.
A program may use at most 256 MiB of HBM per device.

v0:
```python
import math
import jax
import jax.numpy as jnp
from jax import lax
from jax.sharding import PartitionSpec as P

D = 896
HEADS = 14
KV = 2
HEAD = 64
LAYERS = 2
norm_eps = 1e-06
rope_base = 1000000.0


def as_sent(x):

    def short(part):
        return part.astype(jnp.bfloat16) if part.dtype == jnp.float32 else part

    return jax.tree.map(short, x)


def multiply(left_rows, right_matrix, transposed):
    if transposed:
        return lax.dot_general(
            left_rows, right_matrix, (((1,), (1,)), ((), ())), preferred_element_type=jnp.float32
        )
    return jnp.dot(left_rows, right_matrix, preferred_element_type=jnp.float32)


def inner_rows(left_rows, right_rows):
    return lax.dot_general(
        left_rows, right_rows, (((0,), (0,)), ((), ())), preferred_element_type=jnp.float32
    )


def gather_rows(values):
    return lax.all_gather(values, "row", axis=0, tiled=True)


def gather_cols(values):
    return lax.all_gather(values, "col", axis=0, tiled=True)


def reduce_cols(left_rows, right_matrix, transposed):
    share_rows = left_rows.shape[0] // lax.axis_size("col")

    def block_term(start_row, row_count):
        return multiply(left_rows, right_matrix, transposed)

    return lax.psum_scatter(
        block_term(jnp.int32(0), lax.axis_size("col") * share_rows),
        "col",
        scatter_dimension=0,
        tiled=True,
    )


def reduce_rows(left_rows, right_matrix, transposed):
    share_rows = left_rows.shape[0] // lax.axis_size("row")

    def block_term(start_row, row_count):
        return multiply(left_rows, right_matrix, transposed)

    return lax.psum_scatter(
        block_term(jnp.int32(0), lax.axis_size("row") * share_rows),
        "row",
        scatter_dimension=0,
        tiled=True,
    )


def seq_layout(values):
    return lax.all_to_all(values, "row", split_axis=0, concat_axis=1, tiled=True)


def col_layout(values):
    return lax.all_to_all(values, "row", split_axis=1, concat_axis=0, tiled=True)


def width_total(values):
    return lax.psum(values, "col")


def sum_weights(grad_terms):
    return jax.tree.map(lambda part: part.astype(jnp.float32), lax.psum(as_sent(grad_terms), "dp"))


def sum_gains(grad_terms):
    return lax.psum(grad_terms, ("dp", "row"))


def norm_forward(stream, norm_gain):
    squares = width_total(jnp.sum(stream * stream, axis=1))
    inverse = lax.rsqrt(squares / D + norm_eps)
    normed = (stream * inverse[:, None] * norm_gain).astype(jnp.bfloat16)
    return (normed, inverse)


def norm_backward(stream, inverse, norm_gain, grad_normed):
    scaled = stream * inverse[:, None]
    gain_part = jnp.sum(grad_normed * scaled, axis=0)
    weighted = grad_normed * norm_gain
    inner_sum = width_total(jnp.sum(weighted * stream, axis=1))
    grad_stream = (
        weighted * inverse[:, None]
        - stream * (inverse * inverse * inverse * inner_sum / D)[:, None]
    )
    return (grad_stream, gain_part)


def rope_tables(seg_vec):
    index_all = jnp.arange(seg_vec.shape[0], dtype=jnp.int32)
    starts = jnp.concatenate([jnp.ones((1,), jnp.bool_), seg_vec[1:] != seg_vec[:-1]])
    first_idx = lax.cummax(jnp.where(starts, index_all, 0), axis=0)
    positions = (index_all - first_idx).astype(jnp.float32)
    half_dim = HEAD // 2
    freqs = rope_base ** (-(jnp.arange(half_dim, dtype=jnp.float32) * 2.0 / HEAD))
    angles = positions[:, None] * freqs[None, :]
    return (jnp.cos(angles)[:, None, :], jnp.sin(angles)[:, None, :])


def rotate(values, cosine, sine_vals):
    half_dim = values.shape[-1] // 2
    first_half = values[..., :half_dim]
    second_half = values[..., half_dim:]
    return jnp.concatenate(
        [
            first_half * cosine - second_half * sine_vals,
            second_half * cosine + first_half * sine_vals,
        ],
        axis=-1,
    )


def head_layout(qkv_seq, cosine, sine_vals):
    length = qkv_seq.shape[0]
    kv_width = KV * HEAD
    queries = rotate(
        qkv_seq[:, :D].astype(jnp.float32).reshape(length, HEADS, HEAD), cosine, sine_vals
    ).astype(jnp.bfloat16)
    keys_rot = rotate(
        qkv_seq[:, D : D + kv_width].astype(jnp.float32).reshape(length, KV, HEAD),
        cosine,
        sine_vals,
    ).astype(jnp.bfloat16)
    values_all = qkv_seq[:, D + kv_width :].reshape(length, KV, HEAD)
    block_rows = min(length, 512)
    query_blocks = queries.reshape(length // block_rows, block_rows, KV, HEADS // KV, HEAD)
    return (query_blocks, jnp.transpose(keys_rot, (1, 0, 2)), jnp.transpose(values_all, (1, 0, 2)))


def masked_scores(query_blk, keys_t, seg_blk, seg_vec, row_index):
    score_scale = 1.0 / math.sqrt(HEAD)
    col_index = jnp.arange(seg_vec.shape[0], dtype=jnp.int32)
    scores = (
        jnp.einsum("qkgd,ksd->kgqs", query_blk, keys_t, preferred_element_type=jnp.float32)
        * score_scale
    )
    allowed = (seg_blk[:, None] == seg_vec[None, :]) & (row_index[:, None] >= col_index[None, :])
    return jnp.where(allowed[None, None], scores, -1e30)


def attend_forward(qkv_seq, seg_vec, cosine, sine_vals):
    query_blocks, keys_t, values_t = head_layout(qkv_seq, cosine, sine_vals)
    num_blocks = query_blocks.shape[0]
    block_rows = query_blocks.shape[1]
    seg_blocks = seg_vec.reshape(num_blocks, block_rows)
    row_blocks = jnp.arange(seg_vec.shape[0], dtype=jnp.int32).reshape(num_blocks, block_rows)

    def one_block(inputs):
        query_blk, seg_blk, row_index = inputs
        scores = masked_scores(query_blk, keys_t, seg_blk, seg_vec, row_index)
        row_max = jnp.max(scores, axis=-1, keepdims=True)
        exp_scores = jnp.exp(scores - row_max)
        exp_total = jnp.sum(exp_scores, axis=-1, keepdims=True)
        probs = (exp_scores / exp_total).astype(jnp.bfloat16)
        output = jnp.einsum("kgqs,ksd->qkgd", probs, values_t, preferred_element_type=jnp.float32)
        return (
            output.reshape(block_rows, D).astype(jnp.bfloat16),
            (row_max + jnp.log(exp_total))[..., 0],
        )

    outputs, log_norm = lax.map(one_block, (query_blocks, seg_blocks, row_blocks))
    return (outputs.reshape(-1, D), log_norm)


def attend_backward(qkv_seq, seg_vec, cosine, sine_vals, log_norm, grad_attn):
    score_scale = 1.0 / math.sqrt(HEAD)
    query_blocks, keys_t, values_t = head_layout(qkv_seq, cosine, sine_vals)
    num_blocks = query_blocks.shape[0]
    block_rows = query_blocks.shape[1]
    length = seg_vec.shape[0]
    seg_blocks = seg_vec.reshape(num_blocks, block_rows)
    row_blocks = jnp.arange(length, dtype=jnp.int32).reshape(num_blocks, block_rows)
    grad_blocks = grad_attn.reshape(num_blocks, block_rows, KV, HEADS // KV, HEAD)

    def one_block(carry, inputs):
        grad_keys, grad_values = carry
        query_blk, grad_blk, norm_blk, seg_blk, row_index = inputs
        scores = masked_scores(query_blk, keys_t, seg_blk, seg_vec, row_index)
        probs = jnp.exp(scores - norm_blk[..., None])
        grad_probs = jnp.einsum(
            "qkgd,ksd->kgqs", grad_blk, values_t, preferred_element_type=jnp.float32
        )
        inner_sum = jnp.sum(probs * grad_probs, axis=-1, keepdims=True)
        grad_scores = (probs * (grad_probs - inner_sum)).astype(jnp.bfloat16)
        grad_values = grad_values + jnp.einsum(
            "kgqs,qkgd->ksd",
            probs.astype(jnp.bfloat16),
            grad_blk,
            preferred_element_type=jnp.float32,
        )
        grad_keys = (
            grad_keys
            + jnp.einsum(
                "kgqs,qkgd->ksd", grad_scores, query_blk, preferred_element_type=jnp.float32
            )
            * score_scale
        )
        grad_query = (
            jnp.einsum("kgqs,ksd->qkgd", grad_scores, keys_t, preferred_element_type=jnp.float32)
            * score_scale
        )
        return ((grad_keys, grad_values), grad_query)

    zero_keys = jnp.zeros(keys_t.shape, jnp.float32)
    carried, grad_query = lax.scan(
        one_block,
        (zero_keys, zero_keys),
        (query_blocks, grad_blocks, log_norm, seg_blocks, row_blocks),
    )
    grad_keys, grad_values = carried
    grad_query = rotate(grad_query.reshape(length, HEADS, HEAD), cosine, -sine_vals)
    grad_keys = rotate(jnp.transpose(grad_keys, (1, 0, 2)), cosine, -sine_vals)
    grad_values = jnp.transpose(grad_values, (1, 0, 2))
    joined = jnp.concatenate(
        [
            grad_query.reshape(length, D),
            grad_keys.reshape(length, -1),
            grad_values.reshape(length, -1),
        ],
        axis=1,
    )
    return joined.astype(jnp.bfloat16)


def silu_product(gate_part, up_part):
    return jax.nn.silu(gate_part) * up_part


def on_device(
    hidden,
    segments,
    attn_gain,
    qkv_weight,
    qkv_bias,
    out_weight,
    mlp_gain,
    gate_up_weight,
    down_weight,
    cotangent,
):
    seg_vec = segments.reshape(-1)
    cosine, sine_vals = rope_tables(seg_vec)
    stream = hidden.astype(jnp.float32)
    width_dev = gate_up_weight.shape[1]
    saved_layers = []
    for layer_no in range(LAYERS):
        gain_attn = attn_gain[layer_no].astype(jnp.float32)
        gain_mlp = mlp_gain[layer_no].astype(jnp.float32)
        normed_a, inverse_a = norm_forward(stream, gain_attn)
        gathered_a = gather_rows(normed_a)
        qkv_part = reduce_cols(gathered_a, qkv_weight[layer_no], False)
        qkv_cols = (qkv_part + qkv_bias[layer_no].astype(jnp.float32)).astype(jnp.bfloat16)
        qkv_seq = seq_layout(qkv_cols)
        attn_seq, log_norm = attend_forward(qkv_seq, seg_vec, cosine, sine_vals)
        attn_cols = col_layout(attn_seq)
        gathered_o = gather_cols(attn_cols)
        stream_mid = stream + reduce_rows(gathered_o, out_weight[layer_no], False)
        normed_m, inverse_m = norm_forward(stream_mid, gain_mlp)
        gathered_m = gather_rows(normed_m)
        gate_flat = gate_up_weight[layer_no].reshape(width_dev, -1)
        gate_up = reduce_cols(gathered_m, gate_flat, False)
        ff_dev = gate_up.shape[1] // 2
        act_vals = silu_product(gate_up[:, :ff_dev], gate_up[:, ff_dev:]).astype(jnp.bfloat16)
        gathered_h = gather_cols(act_vals)
        stream_next = stream_mid + reduce_rows(gathered_h, down_weight[layer_no], False)
        stored = (gathered_a, gathered_o, gathered_m, gathered_h)
        saved_layers.append(
            (stream, inverse_a, qkv_seq, log_norm, stream_mid, inverse_m, gate_up, stored)
        )
        stream = stream_next
    outcome = stream.astype(jnp.bfloat16)
    grad_stream = cotangent.astype(jnp.float32)
    weight_list = []
    gain_list = []
    for layer_no in reversed(range(LAYERS)):
        stream_in, inverse_a, qkv_seq, log_norm, stream_mid, inverse_m, gate_up, stored = (
            saved_layers[layer_no]
        )
        gain_attn = attn_gain[layer_no].astype(jnp.float32)
        gain_mlp = mlp_gain[layer_no].astype(jnp.float32)
        gate_flat = gate_up_weight[layer_no].reshape(width_dev, -1)
        ff_dev = gate_up.shape[1] // 2
        grad_down = grad_stream.astype(jnp.bfloat16)
        gathered_d = gather_rows(grad_down)
        grad_act = reduce_cols(gathered_d, down_weight[layer_no], True)
        gathered_h = stored[3]
        w_down_grad = inner_rows(gathered_h, gathered_d)
        silu_out, silu_back = jax.vjp(silu_product, gate_up[:, :ff_dev], gate_up[:, ff_dev:])
        grad_gate, grad_up = silu_back(grad_act)
        grad_gu = jnp.concatenate([grad_gate, grad_up], axis=1).astype(jnp.bfloat16)
        gathered_g = gather_cols(grad_gu)
        grad_normed_m = reduce_rows(gathered_g, gate_flat, True)
        gathered_m = stored[2]
        w_gate_grad = inner_rows(gathered_m, gathered_g).reshape(width_dev, 2, ff_dev)
        grad_norm_m, gain_mlp_part = norm_backward(stream_mid, inverse_m, gain_mlp, grad_normed_m)
        grad_mid = grad_stream + grad_norm_m
        grad_out = grad_mid.astype(jnp.bfloat16)
        gathered_y = gather_rows(grad_out)
        grad_attn_cols = reduce_cols(gathered_y, out_weight[layer_no], True)
        gathered_o = stored[1]
        w_out_grad = inner_rows(gathered_o, gathered_y)
        grad_attn_seq = seq_layout(grad_attn_cols.astype(jnp.bfloat16))
        grad_qkv_seq = attend_backward(qkv_seq, seg_vec, cosine, sine_vals, log_norm, grad_attn_seq)
        grad_qkv_cols = col_layout(grad_qkv_seq)
        gathered_q = gather_cols(grad_qkv_cols)
        bias_grad = jnp.sum(gathered_q, axis=0, dtype=jnp.float32)
        grad_normed_a = reduce_rows(gathered_q, qkv_weight[layer_no], True)
        gathered_a = stored[0]
        w_qkv_grad = inner_rows(gathered_a, gathered_q)
        grad_norm_a, gain_attn_part = norm_backward(stream_in, inverse_a, gain_attn, grad_normed_a)
        grad_stream = grad_mid + grad_norm_a
        weight_terms = (w_qkv_grad, bias_grad, w_out_grad, w_gate_grad, w_down_grad)
        gain_terms = (gain_attn_part, gain_mlp_part)
        weight_list.insert(0, weight_terms)
        gain_list.insert(0, gain_terms)
    weight_stack = tuple(
        (jnp.stack([member[index_no] for member in weight_list]) for index_no in range(5))
    )
    gain_stack = tuple(
        (jnp.stack([member[index_no] for member in gain_list]) for index_no in range(2))
    )
    weight_stack = sum_weights(weight_stack)
    gain_stack = sum_gains(gain_stack)
    return (
        outcome,
        grad_stream,
        gain_stack[0],
        weight_stack[0],
        weight_stack[1],
        weight_stack[2],
        gain_stack[1],
        weight_stack[3],
        weight_stack[4],
    )


def solution(mesh):
    in_specs = (
        P(("dp", "row"), "col"),
        P("dp", "col", "row", None),
        P(None, "col"),
        P(None, "col", "row"),
        P(None, "row"),
        P(None, "row", "col"),
        P(None, "col"),
        P(None, "col", None, "row"),
        P(None, "row", "col"),
        P(("dp", "row"), "col"),
    )
    out_specs = (
        P(("dp", "row"), "col"),
        P(("dp", "row"), "col"),
        P(None, "col"),
        P(None, "col", "row"),
        P(None, "row"),
        P(None, "row", "col"),
        P(None, "col"),
        P(None, "col", None, "row"),
        P(None, "row", "col"),
    )
    return jax.shard_map(
        on_device, mesh=mesh, in_specs=in_specs, out_specs=out_specs, check_vma=False
    )
```

profile of v0, /device:TPU:0, one launch (start us, length us, event | category | flops | bytes accessed | tf_op | source)
XLA Modules:
  0.0 2898.2 jit_solution(12900651117420374474)
XLA Ops:
  19.5 41.7 %all-gather.17.cloned.1.call-done = bf16[4096,224]{0,1:T(8,128)(2,1)} async-done(((bf16[1024,224]{0,1:T(8,128)(2,1)}), bf16[4096,224]{0,1:T(8,128)(2,1)}) %all-gather.17.cloned.1.call-update) | async-done | bytes 1835024 | tf_op jit(solution)/shard_map/all_gather | solution.py:39
  67.1 45.5 %reduce-scatter.17.cloned.1.call-done = f32[1024,288]{0,1:T(8,128)} async-done(((f32[4096,288]{0,1:T(8,128)}), f32[1024,288]{0,1:T(8,128)}) %reduce-scatter.17.cloned.1.call-update) | async-done | bytes 1179664 | tf_op jit(solution)/shard_map/reduce_scatter | solution.py:52
  178.8 68.0 %reduce-scatter.19.cloned.1.call-done = f32[1024,224]{0,1:T(8,128)} async-done(((f32[4096,224]{0,1:T(8,128)}), f32[1024,224]{0,1:T(8,128)}) %reduce-scatter.19.cloned.1.call-update) | async-done | bytes 917520 | tf_op jit(solution)/shard_map/reduce_scatter | solution.py:66
  314.3 268.9 %reduce-scatter.21.cloned.1.call-done = f32[1024,2432]{1,0:T(8,128)} async-done(((f32[4096,2432]{1,0:T(8,128)}), f32[1024,2432]{1,0:T(8,128)}) %reduce-scatter.21.cloned.1.call-update) | async-done | bytes 9961488 | tf_op jit(solution)/shard_map/reduce_scatter | solution.py:52
  589.4 70.3 %all-gather.23.cloned.1.call-done = bf16[4096,1216]{1,0:T(8,128)(2,1)} async-done(((bf16[1024,1216]{1,0:T(8,128)(2,1)}), bf16[4096,1216]{1,0:T(8,128)(2,1)}) %all-gather.23.cloned.1.call-update) | async-done | bytes 9961488 | tf_op jit(solution)/shard_map/all_gather | solution.py:43
  668.7 68.6 %reduce-scatter.23.cloned.1.call-done = f32[1024,224]{0,1:T(8,128)} async-done(((f32[4096,224]{0,1:T(8,128)}), f32[1024,224]{0,1:T(8,128)}) %reduce-scatter.23.cloned.1.call-update) | async-done | bytes 917520 | tf_op jit(solution)/shard_map/reduce_scatter | solution.py:66
  745.9 41.4 %all-gather.25.cloned.1.call-done = bf16[4096,224]{0,1:T(8,128)(2,1)} async-done(((bf16[1024,224]{0,1:T(8,128)(2,1)}), bf16[4096,224]{0,1:T(8,128)(2,1)}) %all-gather.25.cloned.1.call-update) | async-done | bytes 1835024 | tf_op jit(solution)/shard_map/all_gather | solution.py:39
  791.9 46.7 %reduce-scatter.25.cloned.1.call-done = f32[1024,288]{0,1:T(8,128)} async-done(((f32[4096,288]{0,1:T(8,128)}), f32[1024,288]{0,1:T(8,128)}) %reduce-scatter.25.cloned.1.call-update) | async-done | bytes 1179664 | tf_op jit(solution)/shard_map/reduce_scatter | solution.py:52
  903.1 67.9 %reduce-scatter.27.cloned.1.call-done = f32[1024,224]{0,1:T(8,128)} async-done(((f32[4096,224]{0,1:T(8,128)}), f32[1024,224]{0,1:T(8,128)}) %reduce-scatter.27.cloned.1.call-update) | async-done | bytes 917520 | tf_op jit(solution)/shard_map/reduce_scatter | solution.py:66
  1083.8 124.4 %reduce-scatter.33.cloned.1.call-done = f32[1024,1216]{1,0:T(8,128)} async-done(((f32[4096,1216]{1,0:T(8,128)}), f32[1024,1216]{1,0:T(8,128)}) %reduce-scatter.33.cloned.1.call-update) | async-done | bytes 4980752 | tf_op jit(solution)/shard_map/reduce_scatter | solution.py:52
  1208.2 272.7 %reduce-scatter.29.cloned.1.call-done = f32[1024,2432]{1,0:T(8,128)} async-done(((f32[4096,2432]{1,0:T(8,128)}), f32[1024,2432]{1,0:T(8,128)}) %reduce-scatter.29.cloned.1.call-update) | async-done | bytes 9961488 | tf_op jit(solution)/shard_map/reduce_scatter | solution.py:52
  1493.0 125.9 %all-gather.35.cloned.1.call-done = bf16[4096,2432]{1,0:T(8,128)(2,1)} async-done(((bf16[1024,2432]{1,0:T(8,128)(2,1)}), bf16[4096,2432]{1,0:T(8,128)(2,1)}) %all-gather.35.cloned.1.call-update) | async-done | bytes 19922960 | tf_op jit(solution)/shard_map/all_gather | solution.py:43
  1633.8 68.6 %reduce-scatter.35.cloned.1.call-done = f32[1024,224]{0,1:T(8,128)} async-done(((f32[4096,224]{0,1:T(8,128)}), f32[1024,224]{0,1:T(8,128)}) %reduce-scatter.35.cloned.1.call-update) | async-done | bytes 917520 | tf_op jit(solution)/shard_map/reduce_scatter | solution.py:66
  1714.7 41.4 %all-gather.37.cloned.1.call-done = bf16[4096,224]{0,1:T(8,128)(2,1)} async-done(((bf16[1024,224]{0,1:T(8,128)(2,1)}), bf16[4096,224]{0,1:T(8,128)(2,1)}) %all-gather.37.cloned.1.call-update) | async-done | bytes 1835024 | tf_op jit(solution)/shard_map/all_gather | solution.py:39
  1873.1 67.0 %all-gather.31.cloned.1.call-done = bf16[4096,1216]{1,0:T(8,128)(2,1)} async-done(((bf16[1024,1216]{1,0:T(8,128)(2,1)}), bf16[4096,1216]{1,0:T(8,128)(2,1)}) %all-gather.31.cloned.1.call-update) | async-done | bytes 9961488 | tf_op jit(solution)/shard_map/all_gather | solution.py:43
  1949.4 62.3 %reduce-scatter.39.cloned.1.call-done = f32[1024,224]{0,1:T(8,128)} async-done(((f32[4096,224]{0,1:T(8,128)}), f32[1024,224]{0,1:T(8,128)}) %reduce-scatter.39.cloned.1.call-update) | async-done | bytes 917520 | tf_op jit(solution)/shard_map/reduce_scatter | solution.py:66
  2019.2 63.4 %reduce-scatter.31.cloned.1.call-done = f32[1024,224]{0,1:T(8,128)} async-done(((f32[4096,224]{0,1:T(8,128)}), f32[1024,224]{0,1:T(8,128)}) %reduce-scatter.31.cloned.1.call-update) | async-done | bytes 917520 | tf_op jit(solution)/shard_map/reduce_scatter | solution.py:66
  2086.2 41.7 %all-gather.41.cloned.1.call-done = bf16[4096,224]{0,1:T(8,128)(2,1)} async-done(((bf16[1024,224]{0,1:T(8,128)(2,1)}), bf16[4096,224]{0,1:T(8,128)(2,1)}) %all-gather.41.cloned.1.call-update) | async-done | bytes 1835024 | tf_op jit(solution)/shard_map/all_gather | solution.py:39
  2139.6 149.3 %reduce-scatter.41.cloned.1.call-done = f32[1024,1216]{1,0:T(8,128)} async-done(((f32[4096,1216]{1,0:T(8,128)}), f32[1024,1216]{1,0:T(8,128)}) %reduce-scatter.41.cloned.1.call-update) | async-done | bytes 4980752 | tf_op jit(solution)/shard_map/reduce_scatter | solution.py:52
  2299.8 125.9 %all-gather.43.cloned.1.call-done = bf16[4096,2432]{1,0:T(8,128)(2,1)} async-done(((bf16[1024,2432]{1,0:T(8,128)(2,1)}), bf16[4096,2432]{1,0:T(8,128)(2,1)}) %all-gather.43.cloned.1.call-update) | async-done | bytes 19922960 | tf_op jit(solution)/shard_map/all_gather | solution.py:43
  2438.0 68.6 %reduce-scatter.43.cloned.1.call-done = f32[1024,224]{0,1:T(8,128)} async-done(((f32[4096,224]{0,1:T(8,128)}), f32[1024,224]{0,1:T(8,128)}) %reduce-scatter.43.cloned.1.call-update) | async-done | bytes 917520 | tf_op jit(solution)/shard_map/reduce_scatter | solution.py:66
  2516.8 41.4 %all-gather.45.cloned.1.call-done = bf16[4096,224]{0,1:T(8,128)(2,1)} async-done(((bf16[1024,224]{0,1:T(8,128)(2,1)}), bf16[4096,224]{0,1:T(8,128)(2,1)}) %all-gather.45.cloned.1.call-update) | async-done | bytes 1835024 | tf_op jit(solution)/shard_map/all_gather | solution.py:39
  2698.3 90.3 %all-reduce.4.cloned.1.call-done = (bf16[2,224,288]{1,2,0:T(8,128)(2,1)}, bf16[2,224,224]{2,1,0:T(8,128)(2,1)}, bf16[2,224,2,1216]{3,2,1,0:T(2,128)(2,1)}, bf16[2,1216,224]{1,2,0:T(8,128)(2,1)}) async-done(((bf16[2,224,288]{1,2,0:T(8,128)(2,1)}, bf16[2,224,224]{2,1,0:T(8,128)(2,1)}, bf16[2,224,2,1216]{3,2,1,0:T(2,128)(2,1)}, bf16[2,1216,224]{1,2,0:T(8,128)(2,1)}), (bf16[2,224,288]{1,2,0:T(8,128)(2,1)}, ...) | async-done | bytes 3727376 | tf_op jit(solution)/shard_map/psum | solution.py:87
  2797.3 62.1 %reduce-scatter.47.cloned.1.call-done = f32[1024,224]{0,1:T(8,128)} async-done(((f32[4096,224]{0,1:T(8,128)}), f32[1024,224]{0,1:T(8,128)}) %reduce-scatter.47.cloned.1.call-update) | async-done | bytes 917520 | tf_op jit(solution)/shard_map/reduce_scatter | solution.py:66
  (405 shorter events, 758.1 us)
Async XLA Ops:
  19.5 93.1 %reduce-scatter.17.cloned.1.call-start = ((), (), s32[]{:S(2)}) async-start(), calls=%async_computation.25 | async-start | bytes 5898240 | tf_op jit(solution)/shard_map/reduce_scatter | solution.py:52
  178.1 118.7 %all-gather.21.cloned.1.call-start = ((), (), s32[]{:S(2)}) async-start(), calls=%async_computation.28 | async-start | bytes 2293760 | tf_op jit(solution)/shard_map/all_gather | solution.py:39
  255.3 327.9 %reduce-scatter.21.cloned.1.call-start = ((), (), s32[]{:S(2)}) async-start(), calls=%async_computation.29 | async-start | bytes 49807360 | tf_op jit(solution)/shard_map/reduce_scatter | solution.py:52
  314.1 345.6 %all-gather.23.cloned.1.call-start = ((), (), s32[]{:S(2)}) async-start(), calls=%async_computation.30 | async-start | bytes 13107200 | tf_op jit(solution)/shard_map/all_gather | solution.py:43
  589.3 148.1 %reduce-scatter.23.cloned.1.call-start = ((), (), s32[]{:S(2)}) async-start(), calls=%async_computation.31 | async-start | bytes 4587520 | tf_op jit(solution)/shard_map/reduce_scatter | solution.py:66
  668.7 118.7 %all-gather.25.cloned.1.call-start = ((), (), s32[]{:S(2)}) async-start(), calls=%async_computation.32 | async-start | bytes 2293760 | tf_op jit(solution)/shard_map/all_gather | solution.py:39
  791.8 106.4 %all-gather.27.cloned.1.call-start = ((), (), s32[]{:S(2)}) async-start(), calls=%async_computation.34 | async-start | bytes 2293760 | tf_op jit(solution)/shard_map/all_gather | solution.py:43
  902.3 111.9 %all-gather.33.cloned.1.call-start = ((), (), s32[]{:S(2)}) async-start(), calls=%async_computation.40 | async-start | bytes 2293760 | tf_op jit(solution)/shard_map/all_gather | solution.py:39
  903.1 153.3 %all-gather.29.cloned.1.call-start = ((), (), s32[]{:S(2)}) async-start(), calls=%async_computation.36 | async-start | bytes 2293760 | tf_op jit(solution)/shard_map/all_gather | solution.py:39
  979.4 228.8 %reduce-scatter.33.cloned.1.call-start = ((), (), s32[]{:S(2)}) async-start(), calls=%async_computation.41 | async-start | bytes 26214400 | tf_op jit(solution)/shard_map/reduce_scatter | solution.py:52
  1026.2 454.7 %reduce-scatter.29.cloned.1.call-start = ((), (), s32[]{:S(2)}) async-start(), calls=%async_computation.37 | async-start | bytes 49807360 | tf_op jit(solution)/shard_map/reduce_scatter | solution.py:52
  1083.8 535.1 %all-gather.35.cloned.1.call-start = ((), (), s32[]{:S(2)}) async-start(), calls=%async_computation.42 | async-start | bytes 24903680 | tf_op jit(solution)/shard_map/all_gather | solution.py:43
  1493.0 209.4 %reduce-scatter.35.cloned.1.call-start = ((), (), s32[]{:S(2)}) async-start(), calls=%async_computation.43 | async-start | bytes 4587520 | tf_op jit(solution)/shard_map/reduce_scatter | solution.py:66
  1633.7 122.4 %all-gather.37.cloned.1.call-start = ((), (), s32[]{:S(2)}) async-start(), calls=%async_computation.44 | async-start | bytes 2293760 | tf_op jit(solution)/shard_map/all_gather | solution.py:39
  1846.1 94.1 %all-gather.31.cloned.1.call-start = ((), (), s32[]{:S(2)}) async-start(), calls=%async_computation.38 | async-start | bytes 13107200 | tf_op jit(solution)/shard_map/all_gather | solution.py:43
  1846.8 164.8 %reduce-scatter.39.cloned.1.call-start = ((), (), s32[]{:S(2)}) async-start(), calls=%async_computation.47 | async-start | bytes 4587520 | tf_op jit(solution)/shard_map/reduce_scatter | solution.py:66
  1873.1 209.6 %reduce-scatter.31.cloned.1.call-start = ((), (), s32[]{:S(2)}) async-start(), calls=%async_computation.39 | async-start | bytes 4587520 | tf_op jit(solution)/shard_map/reduce_scatter | solution.py:66
  1949.3 178.5 %all-gather.41.cloned.1.call-start = ((), (), s32[]{:S(2)}) async-start(), calls=%async_computation.48 | async-start | bytes 2293760 | tf_op jit(solution)/shard_map/all_gather | solution.py:39
  2086.1 202.8 %reduce-scatter.41.cloned.1.call-start = ((), (), s32[]{:S(2)}) async-start(), calls=%async_computation.49 | async-start | bytes 26214400 | tf_op jit(solution)/shard_map/reduce_scatter | solution.py:52
  2139.4 286.2 %all-gather.43.cloned.1.call-start = ((), (), s32[]{:S(2)}) async-start(), calls=%async_computation.50 | async-start | bytes 24903680 | tf_op jit(solution)/shard_map/all_gather | solution.py:43
  2299.7 207.0 %reduce-scatter.43.cloned.1.call-start = ((), (), s32[]{:S(2)}) async-start(), calls=%async_computation.51 | async-start | bytes 4587520 | tf_op jit(solution)/shard_map/reduce_scatter | solution.py:66
  2438.0 120.3 %all-gather.45.cloned.1.call-start = ((), (), s32[]{:S(2)}) async-start(), calls=%async_computation.52 | async-start | bytes 2293760 | tf_op jit(solution)/shard_map/all_gather | solution.py:39
  2651.0 137.6 %all-reduce.4.cloned.1.call-start = ((), (), s32[]{:S(2)}) async-start(), calls=%async_computation.56 | async-start | bytes 7929856 | tf_op jit(solution)/shard_map/psum | solution.py:87
  2684.6 174.7 %reduce-scatter.47.cloned.1.call-start = ((), (), s32[]{:S(2)}) async-start(), calls=%async_computation.55 | async-start | bytes 4587520 | tf_op jit(solution)/shard_map/reduce_scatter | solution.py:66
  (98 other events, 6673.6 us)
Sparse Core Ops, SparseCore 0:
  19.6 41.6 all-gather.16
  66.0 46.5 reduce-scatter.16
  178.3 68.5 reduce-scatter.18
  255.4 41.3 all-gather.20
  314.2 268.9 reduce-scatter.20
  589.5 70.1 all-gather.22
  668.8 68.5 reduce-scatter.22
  792.0 46.5 reduce-scatter.24
  902.4 68.5 reduce-scatter.26
  972.6 41.5 all-gather.32
  1058.8 149.3 reduce-scatter.32
  1210.7 270.1 reduce-scatter.28
  1493.1 125.7 all-gather.34
  1633.8 68.5 reduce-scatter.34
  1870.0 70.1 all-gather.30
  1943.1 68.5 reduce-scatter.38
  2013.8 68.8 reduce-scatter.30
  2086.2 41.5 all-gather.40
  2139.5 149.3 reduce-scatter.40
  2299.8 125.7 all-gather.42
  2438.1 68.5 reduce-scatter.42
  2516.9 41.3 all-gather.44
  2684.7 103.7 all-reduce.3
  2790.7 68.5 reduce-scatter.46
  (9 shorter events, 287.1 us)
where the time goes:
time: 2910 us; the launch traced here: 2900 us
  waiting for transfers between devices  2400 us (82%)
  matrix products  204 us (7%)
  blocking collectives  147 us (5%)
  other arithmetic  90.5 us (3%)
    reduce_scatter x8, waiting for transfers between devices, reduce_cols(): lax.psum_scatter(block_term(jnp.int32(0), lax.axis_size('col') * share_ro...  988 us
    reduce_scatter x8, waiting for transfers between devices, reduce_rows(): lax.psum_scatter(block_term(jnp.int32(0), lax.axis_size('row') * share_ro...  530 us
    all_gather x8, waiting for transfers between devices, gather_cols(): return lax.all_gather(values, 'col', axis=0, tiled=True)  449 us
    all_gather x8, waiting for transfers between devices, gather_rows(): return lax.all_gather(values, 'row', axis=0, tiled=True)  306 us
    psum x1, waiting for transfers between devices, sum_weights(): lax.psum(as_sent(grad_terms), 'dp')  90.3 us
    dot_general x8, matrix products, multiply(): return jnp.dot(left_rows, right_matrix, preferred_element_type=jnp.float32)  79.7 us
    dot_general x8, matrix products, multiply(): lax.dot_general(left_rows, right_matrix, (((1,), (1,)), ((), ())), prefer...  67.9 us
  transfers between devices with their start and end apart: 37, of which 35 were waited for; matrix products, arithmetic and copies ran while one was open for 5% of the time, Pallas kernels for 0%

commit v1 on v0

--- a/solution.py
+++ b/solution.py
@@ -13,6 +13,22 @@
 rope_base = 1000000.0
 
 
+def gather_around(x, axis, dim):
+    ways, here, step = (lax.axis_size(axis), lax.axis_index(axis), x.shape[dim])
+    dims = [n * ways if d == dim else n for d, n in enumerate(x.shape)]
+    full = lax.dynamic_update_slice_in_dim(jnp.zeros(dims, x.dtype), x, here * step, axis=dim)
+    going_up = going_down = x
+    for far in range(1, ways // 2 + 1):
+        going_up = lax.ppermute(going_up, axis, [(d, (d + 1) % ways) for d in range(ways)])
+        full = lax.dynamic_update_slice_in_dim(full, going_up, (here - far) % ways * step, axis=dim)
+        if 2 * far < ways:
+            going_down = lax.ppermute(going_down, axis, [(d, (d - 1) % ways) for d in range(ways)])
+            full = lax.dynamic_update_slice_in_dim(
+                full, going_down, (here + far) % ways * step, axis=dim
+            )
+    return full
+
+
 def as_sent(x):
 
     def short(part):
@@ -36,7 +52,7 @@
 
 
 def gather_rows(values):
-    return lax.all_gather(values, "row", axis=0, tiled=True)
+    return gather_around(values, "row", 0)
 
 
 def gather_cols(values):

time: 2910 us -> 2790 us (0.959)
  waiting for transfers between devices: 2400 us -> 2200 us
  starting transfers between devices: 19.7 us -> 97.4 us
    all_gather x8 -> x0, waiting for transfers between devices: 306 us -> none  [gather_rows(): return lax.all_gather(values, 'row', axis=0, tiled=True)]
    ppermute x0 -> x24, waiting for transfers between devices: none -> 201 us  [the longest x16 171 us: gather_around(): lax.ppermute(going_up, axis, [(d, (d + 1) % ways) for d in range(ways)])]
    ppermute x0 -> x24, starting transfers between devices: none -> 78.1 us  [the longest x16 59.4 us: gather_around(): lax.ppermute(going_up, axis, [(d, (d + 1) % ways) for d in range(ways)])]
    reduce_scatter x8, waiting for transfers between devices: 530 us -> 487 us  [reduce_rows(): lax.psum_scatter(block_term(jnp.int32(0), lax.axis_size('row') * share_ro...]
    reduce_scatter x8, waiting for transfers between devices: 988 us -> 952 us  [reduce_cols(): lax.psum_scatter(block_term(jnp.int32(0), lax.axis_size('col') * share_ro...]
  transfers between devices with their start and end apart: 37 -> 53, of which waited for: 35 -> 50; matrix products, arithmetic and copies ran while one was open for 5% -> 5% of each run, Pallas kernels for 0% -> 0%
where the time goes in v1:
time: 2790 us; the launch traced here: 2780 us
  waiting for transfers between devices  2200 us (79%)
  matrix products  184 us (7%)
  blocking collectives  147 us (5%)
  starting transfers between devices  97.4 us (3%)
  other arithmetic  86.7 us (3%)
  local copies, waits for them, and re-layouts  49.9 us (2%)
    reduce_scatter x8, waiting for transfers between devices, reduce_cols(): lax.psum_scatter(block_term(jnp.int32(0), lax.axis_size('col') * share_ro...  952 us
    reduce_scatter x8, waiting for transfers between devices, reduce_rows(): lax.psum_scatter(block_term(jnp.int32(0), lax.axis_size('row') * share_ro...  487 us
    all_gather x8, waiting for transfers between devices, gather_cols(): return lax.all_gather(values, 'col', axis=0, tiled=True)  439 us
    ppermute x16, waiting for transfers between devices, gather_around(): lax.ppermute(going_up, axis, [(d, (d + 1) % ways) for d in range(ways)])  171 us
    psum x1, waiting for transfers between devices, sum_weights(): lax.psum(as_sent(grad_terms), 'dp')  89.3 us
    dot_general x8, matrix products, multiply(): return jnp.dot(left_rows, right_matrix, preferred_element_type=jnp.float32)  65.5 us
    ppermute x16, starting transfers between devices, gather_around(): lax.ppermute(going_up, axis, [(d, (d + 1) % ways) for d in range(ways)])  59.4 us
    dot_general x8, matrix products, multiply(): lax.dot_general(left_rows, right_matrix, (((1,), (1,)), ((), ())), prefer...  58.7 us
  transfers between devices with their start and end apart: 53, of which 50 were waited for; matrix products, arithmetic and copies ran while one was open for 5% of the time, Pallas kernels for 0%

profile of v1, /device:TPU:0, one launch (start us, length us, event | category | flops | bytes accessed | tf_op | source)
XLA Modules:
  0.0 2781.8 jit_solution(11809535819020160463)
XLA Ops:
  57.0 46.1 %reduce-scatter.17.cloned.1.call-done = f32[1024,288]{0,1:T(8,128)} async-done(((f32[4096,288]{0,1:T(8,128)}), f32[1024,288]{0,1:T(8,128)}) %reduce-scatter.17.cloned.1.call-update) | async-done | bytes 1179664 | tf_op jit(solution)/shard_map/reduce_scatter | solution.py:68
  169.5 68.0 %reduce-scatter.19.cloned.1.call-done = f32[1024,224]{0,1:T(8,128)} async-done(((f32[4096,224]{0,1:T(8,128)}), f32[1024,224]{0,1:T(8,128)}) %reduce-scatter.19.cloned.1.call-update) | async-done | bytes 917520 | tf_op jit(solution)/shard_map/reduce_scatter | solution.py:82
  296.8 269.0 %reduce-scatter.21.cloned.1.call-done = f32[1024,2432]{1,0:T(8,128)} async-done(((f32[4096,2432]{1,0:T(8,128)}), f32[1024,2432]{1,0:T(8,128)}) %reduce-scatter.21.cloned.1.call-update) | async-done | bytes 9961488 | tf_op jit(solution)/shard_map/reduce_scatter | solution.py:68
  571.9 70.3 %all-gather.11.cloned.1.call-done = bf16[4096,1216]{1,0:T(8,128)(2,1)} async-done(((bf16[1024,1216]{1,0:T(8,128)(2,1)}), bf16[4096,1216]{1,0:T(8,128)(2,1)}) %all-gather.11.cloned.1.call-update) | async-done | bytes 9961488 | tf_op jit(solution)/shard_map/all_gather | solution.py:59
  651.3 68.6 %reduce-scatter.23.cloned.1.call-done = f32[1024,224]{0,1:T(8,128)} async-done(((f32[4096,224]{0,1:T(8,128)}), f32[1024,224]{0,1:T(8,128)}) %reduce-scatter.23.cloned.1.call-update) | async-done | bytes 917520 | tf_op jit(solution)/shard_map/reduce_scatter | solution.py:82
  765.6 46.6 %reduce-scatter.25.cloned.1.call-done = f32[1024,288]{0,1:T(8,128)} async-done(((f32[4096,288]{0,1:T(8,128)}), f32[1024,288]{0,1:T(8,128)}) %reduce-scatter.25.cloned.1.call-update) | async-done | bytes 1179664 | tf_op jit(solution)/shard_map/reduce_scatter | solution.py:68
  813.7 20.1 all_to_all.135
  948.5 23.7 reduce-scatter.27.cloned.1.call-done
  1035.5 88.7 %reduce-scatter.33.cloned.1.call-done = f32[1024,1216]{1,0:T(8,128)} async-done(((f32[4096,1216]{1,0:T(8,128)}), f32[1024,1216]{1,0:T(8,128)}) %reduce-scatter.33.cloned.1.call-update) | async-done | bytes 4980752 | tf_op jit(solution)/shard_map/reduce_scatter | solution.py:68
  1124.2 272.8 %reduce-scatter.29.cloned.1.call-done = f32[1024,2432]{1,0:T(8,128)} async-done(((f32[4096,2432]{1,0:T(8,128)}), f32[1024,2432]{1,0:T(8,128)}) %reduce-scatter.29.cloned.1.call-update) | async-done | bytes 9961488 | tf_op jit(solution)/shard_map/reduce_scatter | solution.py:68
  1412.6 64.0 %all-gather.15.cloned.1.call-done = bf16[4096,1216]{1,0:T(8,128)(2,1)} async-done(((bf16[1024,1216]{1,0:T(8,128)(2,1)}), bf16[4096,1216]{1,0:T(8,128)(2,1)}) %all-gather.15.cloned.1.call-update) | async-done | bytes 9961488 | tf_op jit(solution)/shard_map/all_gather | solution.py:59
  1486.3 117.7 %all-gather.17.cloned.1.call-done = bf16[4096,2432]{1,0:T(8,128)(2,1)} async-done(((bf16[1024,2432]{1,0:T(8,128)(2,1)}), bf16[4096,2432]{1,0:T(8,128)(2,1)}) %all-gather.17.cloned.1.call-update) | async-done | bytes 19922960 | tf_op jit(solution)/shard_map/all_gather | solution.py:59
  1618.9 55.8 %reduce-scatter.31.cloned.1.call-done = f32[1024,224]{0,1:T(8,128)} async-done(((f32[4096,224]{0,1:T(8,128)}), f32[1024,224]{0,1:T(8,128)}) %reduce-scatter.31.cloned.1.call-update) | async-done | bytes 917520 | tf_op jit(solution)/shard_map/reduce_scatter | solution.py:82
  1674.7 71.6 %reduce-scatter.35.cloned.1.call-done = f32[1024,224]{0,1:T(8,128)} async-done(((f32[4096,224]{0,1:T(8,128)}), f32[1024,224]{0,1:T(8,128)}) %reduce-scatter.35.cloned.1.call-update) | async-done | bytes 917520 | tf_op jit(solution)/shard_map/reduce_scatter | solution.py:82
  1794.6 39.9 %reduce-scatter.37.cloned.1.call-done = f32[1024,224]{0,1:T(8,128)} async-done(((f32[4096,224]{0,1:T(8,128)}), f32[1024,224]{0,1:T(8,128)}) %reduce-scatter.37.cloned.1.call-update) | async-done | bytes 917520 | tf_op jit(solution)/shard_map/reduce_scatter | solution.py:68
  1881.1 22.3 all-gather.19.cloned.1.call-done
  1908.1 68.6 %reduce-scatter.39.cloned.1.call-done = f32[1024,224]{0,1:T(8,128)} async-done(((f32[4096,224]{0,1:T(8,128)}), f32[1024,224]{0,1:T(8,128)}) %reduce-scatter.39.cloned.1.call-update) | async-done | bytes 917520 | tf_op jit(solution)/shard_map/reduce_scatter | solution.py:82
  2030.4 149.5 %reduce-scatter.41.cloned.1.call-done = f32[1024,1216]{1,0:T(8,128)} async-done(((f32[4096,1216]{1,0:T(8,128)}), f32[1024,1216]{1,0:T(8,128)}) %reduce-scatter.41.cloned.1.call-update) | async-done | bytes 4980752 | tf_op jit(solution)/shard_map/reduce_scatter | solution.py:68
  2190.7 125.9 %all-gather.21.cloned.1.call-done = bf16[4096,2432]{1,0:T(8,128)(2,1)} async-done(((bf16[1024,2432]{1,0:T(8,128)(2,1)}), bf16[4096,2432]{1,0:T(8,128)(2,1)}) %all-gather.21.cloned.1.call-update) | async-done | bytes 19922960 | tf_op jit(solution)/shard_map/all_gather | solution.py:59
  2329.0 68.6 %reduce-scatter.43.cloned.1.call-done = f32[1024,224]{0,1:T(8,128)} async-done(((f32[4096,224]{0,1:T(8,128)}), f32[1024,224]{0,1:T(8,128)}) %reduce-scatter.43.cloned.1.call-update) | async-done | bytes 917520 | tf_op jit(solution)/shard_map/reduce_scatter | solution.py:82
  2444.5 39.2 %reduce-scatter.45.cloned.1.call-done = f32[1024,224]{0,1:T(8,128)} async-done(((f32[4096,224]{0,1:T(8,128)}), f32[1024,224]{0,1:T(8,128)}) %reduce-scatter.45.cloned.1.call-update) | async-done | bytes 917520 | tf_op jit(solution)/shard_map/reduce_scatter | solution.py:68
  2584.0 89.3 %all-reduce.4.cloned.1.call-done = (bf16[2,224,288]{1,2,0:T(8,128)(2,1)}, bf16[2,224,224]{2,1,0:T(8,128)(2,1)}, bf16[2,224,2,1216]{3,2,1,0:T(2,128)(2,1)}, bf16[2,1216,224]{1,2,0:T(8,128)(2,1)}) async-done(((bf16[2,224,288]{1,2,0:T(8,128)(2,1)}, bf16[2,224,224]{2,1,0:T(8,128)(2,1)}, bf16[2,224,2,1216]{3,2,1,0:T(2,128)(2,1)}, bf16[2,1216,224]{1,2,0:T(8,128)(2,1)}), (bf16[2,224,288]{1,2,0:T(8,128)(2,1)}, ...) | async-done | bytes 3727376 | tf_op jit(solution)/shard_map/psum | solution.py:103
  2682.0 62.2 %reduce-scatter.47.cloned.1.call-done = f32[1024,224]{0,1:T(8,128)} async-done(((f32[4096,224]{0,1:T(8,128)}), f32[1024,224]{0,1:T(8,128)}) %reduce-scatter.47.cloned.1.call-update) | async-done | bytes 917520 | tf_op jit(solution)/shard_map/reduce_scatter | solution.py:82
  2752.0 21.6 all-reduce
  (492 shorter events, 795.4 us)
Async XLA Ops:
  7.2 95.9 %reduce-scatter.17.cloned.1.call-start = ((), (), s32[]{:S(2)}) async-start(), calls=%async_computation.24 | async-start | bytes 5898240 | tf_op jit(solution)/shard_map/reduce_scatter | solution.py:68
  109.9 54.9 %all-gather.9.cloned.1.call-start = ((), (), s32[]{:S(2)}) async-start(), calls=%async_computation.25 | async-start | bytes 2293760 | tf_op jit(solution)/shard_map/all_gather | solution.py:59
  145.4 92.1 %reduce-scatter.19.cloned.1.call-start = ((), (), s32[]{:S(2)}) async-start(), calls=%async_computation.26 | async-start | bytes 4587520 | tf_op jit(solution)/shard_map/reduce_scatter | solution.py:82
  168.8 396.9 %reduce-scatter.21.cloned.1.call-start = ((), (), s32[]{:S(2)}) async-start(), calls=%async_computation.27 | async-start | bytes 49807360 | tf_op jit(solution)/shard_map/reduce_scatter | solution.py:68
  296.5 345.7 %all-gather.11.cloned.1.call-start = ((), (), s32[]{:S(2)}) async-start(), calls=%async_computation.28 | async-start | bytes 13107200 | tf_op jit(solution)/shard_map/all_gather | solution.py:59
  571.9 148.1 %reduce-scatter.23.cloned.1.call-start = ((), (), s32[]{:S(2)}) async-start(), calls=%async_computation.29 | async-start | bytes 4587520 | tf_op jit(solution)/shard_map/reduce_scatter | solution.py:82
  651.2 161.0 %reduce-scatter.25.cloned.1.call-start = ((), (), s32[]{:S(2)}) async-start(), calls=%async_computation.30 | async-start | bytes 5898240 | tf_op jit(solution)/shard_map/reduce_scatter | solution.py:68
  765.6 107.8 %all-gather.13.cloned.1.call-start = ((), (), s32[]{:S(2)}) async-start(), calls=%async_computation.31 | async-start | bytes 2293760 | tf_op jit(solution)/shard_map/all_gather | solution.py:59
  854.0 118.3 %reduce-scatter.27.cloned.1.call-start = ((), (), s32[]{:S(2)}) async-start(), calls=%async_computation.32 | async-start | bytes 4587520 | tf_op jit(solution)/shard_map/reduce_scatter | solution.py:82
  877.4 246.9 %reduce-scatter.33.cloned.1.call-start = ((), (), s32[]{:S(2)}) async-start(), calls=%async_computation.36 | async-start | bytes 26214400 | tf_op jit(solution)/shard_map/reduce_scatter | solution.py:68
  948.5 448.6 %reduce-scatter.29.cloned.1.call-start = ((), (), s32[]{:S(2)}) async-start(), calls=%async_computation.33 | async-start | bytes 49807360 | tf_op jit(solution)/shard_map/reduce_scatter | solution.py:68
  1035.5 441.2 %all-gather.15.cloned.1.call-start = ((), (), s32[]{:S(2)}) async-start(), calls=%async_computation.34 | async-start | bytes 13107200 | tf_op jit(solution)/shard_map/all_gather | solution.py:59
  1406.3 197.7 %all-gather.17.cloned.1.call-start = ((), (), s32[]{:S(2)}) async-start(), calls=%async_computation.37 | async-start | bytes 24903680 | tf_op jit(solution)/shard_map/all_gather | solution.py:59
  1412.5 262.2 %reduce-scatter.31.cloned.1.call-start = ((), (), s32[]{:S(2)}) async-start(), calls=%async_computation.35 | async-start | bytes 4587520 | tf_op jit(solution)/shard_map/reduce_scatter | solution.py:82
  1485.8 260.5 %reduce-scatter.35.cloned.1.call-start = ((), (), s32[]{:S(2)}) async-start(), calls=%async_computation.38 | async-start | bytes 4587520 | tf_op jit(solution)/shard_map/reduce_scatter | solution.py:82
  1618.9 215.7 %reduce-scatter.37.cloned.1.call-start = ((), (), s32[]{:S(2)}) async-start(), calls=%async_computation.39 | async-start | bytes 4587520 | tf_op jit(solution)/shard_map/reduce_scatter | solution.py:68
  1841.2 62.1 %all-gather.19.cloned.1.call-start = ((), (), s32[]{:S(2)}) async-start(), calls=%async_computation.40 | async-start | bytes 2949120 | tf_op jit(solution)/shard_map/all_gather | solution.py:59
  1881.0 95.7 %reduce-scatter.39.cloned.1.call-start = ((), (), s32[]{:S(2)}) async-start(), calls=%async_computation.41 | async-start | bytes 4587520 | tf_op jit(solution)/shard_map/reduce_scatter | solution.py:82
  1908.1 271.8 %reduce-scatter.41.cloned.1.call-start = ((), (), s32[]{:S(2)}) async-start(), calls=%async_computation.42 | async-start | bytes 26214400 | tf_op jit(solution)/shard_map/reduce_scatter | solution.py:68
  2030.3 286.2 %all-gather.21.cloned.1.call-start = ((), (), s32[]{:S(2)}) async-start(), calls=%async_computation.43 | async-start | bytes 24903680 | tf_op jit(solution)/shard_map/all_gather | solution.py:59
  2190.6 207.0 %reduce-scatter.43.cloned.1.call-start = ((), (), s32[]{:S(2)}) async-start(), calls=%async_computation.44 | async-start | bytes 4587520 | tf_op jit(solution)/shard_map/reduce_scatter | solution.py:82
  2328.9 154.8 %reduce-scatter.45.cloned.1.call-start = ((), (), s32[]{:S(2)}) async-start(), calls=%async_computation.45 | async-start | bytes 4587520 | tf_op jit(solution)/shard_map/reduce_scatter | solution.py:68
  2535.0 138.3 %all-reduce.4.cloned.1.call-start = ((), (), s32[]{:S(2)}) async-start(), calls=%async_computation.48 | async-start | bytes 7929856 | tf_op jit(solution)/shard_map/psum | solution.py:103
  2569.7 174.5 %reduce-scatter.47.cloned.1.call-start = ((), (), s32[]{:S(2)}) async-start(), calls=%async_computation.47 | async-start | bytes 4587520 | tf_op jit(solution)/shard_map/reduce_scatter | solution.py:82
  (129 other events, 5714.1 us)
Sparse Core Ops, SparseCore 0:
  55.8 47.1 reduce-scatter.16
  169.0 68.5 reduce-scatter.18
  296.6 269.0 reduce-scatter.20
  572.0 70.1 all-gather.10
  651.3 68.5 reduce-scatter.22
  765.7 46.5 reduce-scatter.24
  854.1 19.2 all-gather.12
  877.5 94.6 reduce-scatter.26
  974.7 149.5 reduce-scatter.32
  1126.8 270.1 reduce-scatter.28
  1406.4 70.1 all-gather.14
  1478.2 125.7 all-gather.16
  1606.2 68.5 reduce-scatter.30
  1677.5 68.8 reduce-scatter.34
  1794.7 39.7 reduce-scatter.36
  1881.1 22.1 all-gather.18
  1908.1 68.5 reduce-scatter.38
  2030.5 149.3 reduce-scatter.40
  2190.7 125.7 all-gather.20
  2329.0 68.5 reduce-scatter.42
  2443.9 39.7 reduce-scatter.44
  2535.1 24.4 all-gather.22
  2569.8 103.4 all-reduce.3
  2675.6 68.5 reduce-scatter.46
  (1 shorter events, 19.2 us)
